TPU v7x, 256 devices: a whole 4x4x8 slice. The times are simulated.
256 devices in a mesh: leaf: 16 (over x, y), blk: 16 (over z, core).
Axes of the slice: x: 4, y: 4, z: 8, core: 2. Of those that a mesh axis runs over, the one named last changes fastest.
Arguments:
- near_tiles: bfloat16 [128, 16, 512, 512], P('leaf', 'blk'), may hold values from -0.25 to 0.25
- near_cols: int32 [128, 16], P('leaf', 'blk'), may hold values from 0 to 127, as said below
- near_count: int32 [128], P('leaf'), may hold values from 1 to 16, as said below
- probes: bfloat16 [128, 512, 512], P('leaf'), may hold values from -6 to 6
- mixing: float32 [512, 64], replicated, may hold values from -0.25 to 0.25
- far_tiles: bfloat16 [128, 16, 512, 512], P('leaf', 'blk'), may hold values from -6 to 6
- far_cols: int32 [128, 16], P('leaf', 'blk'), may hold values from 0 to 127, as said below
Outputs:
- coupling: float32 [128, 16, 64, 64], P('leaf', 'blk')
- root_part: float32 [128, 64, 64], P('leaf')
Inputs may be any that keep to these rules, and one draw needn't show every extreme that they name: near_cols[r, k] lies within 8 of r; the slots below near_count[r] name distinct clusters. Slots at or past near_count[r] hold arbitrary tiles that must be ignored. far_cols[r, j] differs from r by more than 8.
All inputs are finite; a program needn't handle non-finite values.
Results may differ from a plain program's by a relative error of at most 0.0041.
Values may be sent and summed in bfloat16 or wider, within the bound.
No kernel may reach another device: no remote copies, remote signals or barrier semaphores. Data moves between devices by JAX's collectives and lax.ppermute only.
A program may use at most 128 MiB of HBM per device.

v0:
```python
import math
import jax
import jax.numpy as jnp
from jax import lax
from jax.sharding import PartitionSpec as P

RANK = 64
REACH = 8
highest = lax.Precision.HIGHEST


def padded(value, sides, width):
    for axis, dim in sides:
        peers, length = (lax.axis_size(axis), value.shape[dim])
        up = [(i, (i + 1) % peers) for i in range(peers - 1)]
        down = [(j, i) for i, j in up]
        last = lax.slice_in_dim(value, length - width, length, axis=dim)
        leading = lax.slice_in_dim(value, 0, width, axis=dim)
        before = lax.ppermute(last, axis, up)
        after = lax.ppermute(leading, axis, down)
        value = jnp.concatenate([before, value, after], axis=dim)
    return value


def partner_2(block, axis, apart):
    count = lax.axis_size(axis)
    route = []
    for low in range(count):
        high = low | 1 << apart
        if high != low and high < count:
            route += [(low, high), (high, low)]
    return lax.ppermute(block, axis, route)


def basis_from(gram_matrix, mixed_rows):
    lower_factor = jnp.linalg.cholesky(gram_matrix)
    solved = jax.scipy.linalg.solve_triangular(
        lower_factor, jnp.swapaxes(mixed_rows, -1, -2), lower=True
    )
    return jnp.swapaxes(solved, -1, -2)


def merge(stacked, mixing):
    mixed_rows = jnp.einsum("...mp,pk->...mk", stacked, mixing, precision=highest)
    gram_matrix = jnp.einsum("...mk,...ml->...kl", mixed_rows, mixed_rows, precision=highest)
    transfer = basis_from(gram_matrix, mixed_rows)
    merged = jnp.einsum("...mk,...mp->...kp", transfer, stacked, precision=highest)
    return (transfer, merged)


def shards(near_tiles, near_cols, near_count, probes, mixing, far_tiles, far_cols):
    local_rows = probes.shape[0]
    near_dev = near_tiles.shape[1]
    leaf_pos = lax.axis_index("leaf")
    blk_pos = lax.axis_index("blk")
    subtrees = lax.axis_size("leaf")
    clusters = local_rows * subtrees
    first_cluster = leaf_pos * local_rows - REACH
    window = padded(probes, (("leaf", 0),), REACH)

    def leaf_sketch(row_index):
        running = jnp.zeros((probes.shape[1], probes.shape[2]), jnp.float32)
        column = near_cols[row_index, 0] - first_cluster
        probe_block = lax.dynamic_index_in_dim(window, column, 0, keepdims=False)
        near_tile = near_tiles[row_index, 0]
        is_live = blk_pos * near_dev + 0 < near_count[row_index]
        running = lax.cond(
            is_live,
            lambda current: jnp.dot(near_tile, probe_block, preferred_element_type=jnp.float32),
            lambda current: current,
            running,
        )
        return running

    partial_sketch = lax.map(leaf_sketch, jnp.arange(local_rows))
    sketch_rows = lax.psum_scatter(partial_sketch, "blk", scatter_dimension=1, tiled=True)
    mixed_rows = jnp.einsum("rbp,pk->rbk", sketch_rows, mixing, precision=highest)
    gram_part = jnp.einsum("rbk,rbl->rkl", mixed_rows, mixed_rows, precision=highest)
    gram_matrix = lax.psum(gram_part, "blk")
    basis_part = basis_from(gram_matrix, mixed_rows)
    proj_part = jnp.einsum("rbk,rbp->rkp", basis_part, sketch_rows, precision=highest)
    leaf_proj = lax.psum(proj_part, "blk")
    basis_low = lax.all_gather(basis_part.astype(jnp.bfloat16), "blk", axis=1, tiled=True)
    all_bases = lax.all_gather(basis_low, "leaf", axis=0, tiled=True)
    far_basis = all_bases[far_cols]
    far_image = jnp.einsum(
        "rjab,rjbk->rjak", far_tiles, far_basis, preferred_element_type=jnp.float32
    )
    coupling = jnp.einsum(
        "rak,rjal->rjkl", basis_low.astype(jnp.float32), far_image, precision=highest
    )
    sub_stack = leaf_proj.reshape(local_rows * RANK, leaf_proj.shape[2])
    sub_transfer, node_sketch = merge(sub_stack, mixing)
    levels = subtrees.bit_length() - 1
    path_factor = jnp.eye(RANK, dtype=jnp.float32)
    for depth_index in range(levels):
        partner = partner_2(node_sketch.astype(jnp.bfloat16), "leaf", depth_index).astype(
            node_sketch.dtype
        )
        is_upper = leaf_pos >> depth_index & 1
        lower_half = jnp.where(is_upper == 1, partner, node_sketch)
        upper_half = jnp.where(is_upper == 1, node_sketch, partner)
        transfer, node_sketch = merge(jnp.concatenate([lower_half, upper_half], 0), mixing)
        picked = lax.dynamic_slice_in_dim(transfer, is_upper * RANK, RANK, 0)
        path_factor = jnp.dot(path_factor, picked, precision=highest)
    sub_blocks = sub_transfer.reshape(local_rows, RANK, RANK)
    root_part = jnp.einsum("cab,bd->cad", sub_blocks, path_factor, precision=highest)
    root_part = root_part * math.sqrt(clusters * RANK)
    return (coupling, root_part)


def solution(mesh):
    in_specs = (
        P("leaf", "blk", None, None),
        P("leaf", "blk"),
        P("leaf"),
        P("leaf", None, None),
        P(),
        P("leaf", "blk", None, None),
        P("leaf", "blk"),
    )
    out_specs = (P("leaf", "blk", None, None), P("leaf", None, None))
    return jax.shard_map(shards, mesh=mesh, in_specs=in_specs, out_specs=out_specs, check_vma=False)
```

profile of v0, /device:TPU:22, one launch (start us, length us, event | category | flops | bytes accessed | tf_op | source)
XLA Modules:
  0.0 679.8 jit_solution(7134080984132930772)
XLA Ops:
  7.2 3.2 collective-permute-start
  10.4 2.7 collective-permute-start.1
  13.1 88.6 %collective-permute-done = bf16[8,512,512]{2,1,0:T(8,128)(2,1)} collective-permute-done((bf16[8,512,512]{2,1,0:T(8,128)(2,1)}, bf16[8,512,512]{2,1,0:T(8,128)(2,1)}, u32[]{:S(2)}, u32[]{:S(2)}) %collective-permute-start) | collective-permute-done | bytes 4194336 | tf_op jit(solution)/shard_map/ppermute | solution.py:19
  101.7 2.9 collective-permute-done.1
  104.7 10.8 %pad_maximum_fusion = bf16[24,512,512]{2,1,0:T(8,128)(2,1)} fusion(bf16[8,512,512]{2,1,0:T(8,128)(2,1)} %collective-permute-done.1, bf16[8,512,512]{2,1,0:T(8,128)(2,1)} %param.17, bf16[8,512,512]{2,1,0:T(8,128)(2,1)} %collective-permute-done), kind=kLoop, calls=%fused_computation.9 | loop fusion | flops 12582912 | bytes 25165824 | tf_op jit(solution)/shard_map/concatenate | solution.py:21
  115.4 60.4 %while.10 = (s32[]{:T(128)}, f32[8,512,512]{2,1,0:T(8,128)}, s32[8]{0:T(128)S(1)}, s32[8]{0:T(128)S(1)}, s32[]{:T(128)}, /*index=5*/bf16[8,1,512,512]{3,2,1,0:T(...) while((s32[]{:T(128)}, f32[8,512,512]{2,1,0:T(8,128)}, ...), condition=%wide.region_3.4_spmd, body=%wide.region_0.3_spmd.sunk | while | flops 268435456 | bytes 4195627 | solution.py:75
  119.1 2.8 conditional.2
  120.3 1.6 convolution_bitcast_fusion
  121.9 1.1 constant_dynamic-update-slice_fusion.2
  126.7 2.8 conditional.2
  127.9 1.6 convolution_bitcast_fusion
  129.5 1.0 constant_dynamic-update-slice_fusion.2
  134.2 2.8 conditional.2
  135.4 1.6 convolution_bitcast_fusion
  137.0 1.1 constant_dynamic-update-slice_fusion.2
  141.7 2.8 conditional.2
  142.9 1.6 convolution_bitcast_fusion
  144.5 1.1 constant_dynamic-update-slice_fusion.2
  149.3 2.8 conditional.2
  150.4 1.6 convolution_bitcast_fusion
  152.1 1.1 constant_dynamic-update-slice_fusion.2
  156.8 2.8 conditional.2
  158.0 1.6 convolution_bitcast_fusion
  159.6 1.1 constant_dynamic-update-slice_fusion.2
  164.4 2.8 conditional.2
  165.6 1.6 convolution_bitcast_fusion
  167.2 1.1 constant_dynamic-update-slice_fusion.2
  171.9 2.8 conditional.2
  173.1 1.6 convolution_bitcast_fusion
  174.7 1.1 constant_dynamic-update-slice_fusion.2
  175.9 75.0 %reduce-scatter.2.cloned.1.call-done = f32[8,32,512]{2,1,0:T(8,128)} async-done(((f32[8,512,512]{2,1,0:T(8,128)}), f32[8,32,512]{2,1,0:T(8,128)}) %reduce-scatter.2.cloned.1.call-update) | async-done | bytes 524304 | tf_op jit(solution)/shard_map/reduce_scatter | solution.py:76
  250.8 1.6 fusion.20
  252.5 1.3 fusion.69
  253.9 108.8 %all-reduce.3.cloned.1.call-done = f32[8,64,64]{1,2,0:T(8,128)} async-done(((f32[8,64,64]{1,2,0:T(8,128)}), f32[8,64,64]{1,2,0:T(8,128)}) %all-reduce.3.cloned.1.call-update) | async-done | bytes 131088 | tf_op jit(solution)/shard_map/psum | solution.py:79
  362.7 1.1 copy.31
  363.8 1.0 fusion.13
  364.8 46.9 %custom-call.17 = f32[8,64,64]{2,1,0:T(8,128)S(1)} custom-call(f32[8,64,64]{2,1,0:T(8,128)S(1)} %fusion.13), custom_call_target="Cholesky" | custom-call | tf_op jit(solution)/shard_map/jit(cholesky)/cholesky | solution.py:36
  411.9 39.3 %custom-call.18 = f32[8,1,64,64]{2,3,1,0:T(8,128)S(1)} custom-call(f32[8,1,64,64]{3,2,1,0:T(8,128)S(1)} %select_bitcast_fusion), custom_call_target="InvertDiagBlocksLowerTriangular" | custom-call | tf_op jit(solution)/shard_map/jit(_solve_triangular)/vmap()/triangular_solve | solution.py:37
  451.6 3.1 fusion.70
  454.9 18.4 %all_gather.6 = bf16[8,512,64]{2,1,0:T(8,128)(2,1)S(1)} all-gather(bf16[8,32,64]{2,1,0:T(8,128)(2,1)S(1)} %convert_bitcast_fusion), channel_id=1, replica_groups=mesh['leaf'=16,'blk'=16] {'blk'}, dimensions={1}, use_global_device_ids=true | all-gather | bytes 557056 | tf_op jit(solution)/shard_map/all_gather | solution.py:83
  473.3 1.2 copy.33
  474.5 93.2 %all-reduce.5.cloned.1.call-done = f32[512,512]{1,0:T(8,128)} async-done(((f32[512,512]{1,0:T(8,128)}), f32[512,512]{1,0:T(8,128)}) %all-reduce.5.cloned.1.call-update) | async-done | bytes 1048592 | tf_op jit(solution)/shard_map/psum | solution.py:82
  567.8 2.4 fusion.71
  570.5 5.8 cholesky.127
  577.7 4.9 custom-call.19
  582.9 2.0 fusion.65
  584.9 1.5 collective-permute-start.2
  586.5 4.7 collective-permute-done.2
  591.9 5.8 cholesky.138
  599.1 4.9 custom-call.23
  605.3 5.9 collective-permute-done.3
  611.9 5.8 cholesky.149
  619.1 4.9 custom-call.24
  625.4 5.0 collective-permute-done.4
  631.1 5.8 cholesky.160
  638.3 4.9 custom-call.25
  643.7 1.6 collective-permute-start.5
  645.6 4.3 collective-permute-done.5
  650.5 5.8 cholesky.171
  657.7 4.9 custom-call.26
  663.1 1.1 convolution_multiply_fusion
  664.2 4.0 gather_fusion
  668.2 3.6 fusion.5
  672.4 0.8 copy.40
  (106 shorter events, 29.9 us)
Async XLA Ops:
  7.2 243.7 %copy-start = (f32[512,64]{0,1:T(8,128)S(1)}, f32[512,64]{0,1:T(8,128)}, u32[]{:S(2)}) copy-start(f32[512,64]{0,1:T(8,128)} %param.18) | copy-start | bytes 393220
  7.2 243.7 %reduce-scatter.2.cloned.1.call-start = ((), (), s32[]{:S(2)}) async-start(), calls=%async_computation.1 | async-start | bytes 8912896 | tf_op jit(solution)/shard_map/reduce_scatter | solution.py:76
  7.2 94.5 %collective-permute-start = (bf16[8,512,512]{2,1,0:T(8,128)(2,1)}, bf16[8,512,512]{2,1,0:T(8,128)(2,1)}, u32[]{:S(2)}, u32[]{:S(2)}) collective-permute-start(bf16[8,512,512]{2,1,0:T(8,128)(2,1)} %param.17), channel_id=1, source_target_pairs={{0,16},{16,32},{32,48},{48,64},{64,80},{80,96},{96,112},{112,128},... | collective-permute-start | bytes 12582920 | tf_op jit(solution)/shard_map/ppermute | solution.py:19
  10.4 94.2 %collective-permute-start.1 = (bf16[8,512,512]{2,1,0:T(8,128)(2,1)}, bf16[8,512,512]{2,1,0:T(8,128)(2,1)}, u32[]{:S(2)}, u32[]{:S(2)}) collective-permute-start(bf16[8,512,512]{2,1,0:T(8,128)(2,1)} %param.17), channel_id=1, source_target_pairs={{16,0},{32,16},{48,32},{64,48},{80,64},{96,80},{112,96},{128,112},... | collective-permute-start | bytes 12582920 | tf_op jit(solution)/shard_map/ppermute | solution.py:20
  13.1 102.3 %copy-start.1 = (s32[8]{0:T(128)S(1)}, s32[8]{0:T(128)}, u32[]{:S(2)}) copy-start(s32[8]{0:T(128)} %param.16) | copy-start | bytes 100
  13.1 102.3 %copy-start.2 = (s32[8,1]{0,1:T(1,128)S(1)}, s32[8,1]{0,1:T(1,128)}, u32[]{:S(2)}) copy-start(s32[8,1]{0,1:T(1,128)} %param.15) | copy-start | bytes 100
  175.8 298.7 %copy-start.3 = (s32[8,1]{0,1:T(1,128)S(1)}, s32[8,1]{0,1:T(1,128)}, u32[]{:S(2)}) copy-start(s32[8,1]{0,1:T(1,128)} %param.20) | copy-start | bytes 100
  175.8 186.9 %all-reduce.3.cloned.1.call-start = ((), (), s32[]{:S(2)}) async-start(), calls=%async_computation.2 | async-start | bytes 524288 | tf_op jit(solution)/shard_map/psum | solution.py:79
  253.8 314.0 %all-reduce.5.cloned.1.call-start = ((), (), s32[]{:S(2)}) async-start(), calls=%async_computation.4 | async-start | bytes 2097152 | tf_op jit(solution)/shard_map/psum | solution.py:82
  454.8 209.4 %all-gather.2.cloned.1.call-start = ((), (), s32[]{:S(2)}) async-start(), calls=%async_computation.3 | async-start | bytes 8912896 | tf_op jit(solution)/shard_map/all_gather | solution.py:84
  584.9 6.3 collective-permute-start.2
  604.5 6.7 collective-permute-start.3
  624.5 5.9 collective-permute-start.4
  643.7 6.1 collective-permute-start.5
Sparse Core Ops, SparseCore 0:
  175.9 74.8 reduce-scatter.1
  253.9 108.7 all-reduce.2
  454.9 112.7 all-reduce.4
  570.0 76.4 all-gather.1
where the time goes:
time: 681 us; the launch traced here: 680 us
  waiting for transfers between devices  388 us (57%)
  other arithmetic  159 us (23%)
  matrix products  35 us (5%)
  local copies, waits for them, and re-layouts  30.2 us (4%)
  loops' own time  24.6 us (4%)
  blocking collectives  18.4 us (3%)
  between operations  14.2 us (2%)
  starting transfers between devices  10.2 us (1%)
    psum x1, waiting for transfers between devices, shards(): gram_matrix = lax.psum(gram_part, 'blk')  109 us
    psum x1, waiting for transfers between devices, shards(): leaf_proj = lax.psum(proj_part, 'blk')  93.2 us
    ppermute x1, waiting for transfers between devices, padded(): before = lax.ppermute(last, axis, up)  88.6 us
    another operation x19, other arithmetic, basis_from(): lower_factor = jnp.linalg.cholesky(gram_matrix)  79.7 us
    reduce_scatter x1, waiting for transfers between devices, shards(): lax.psum_scatter(partial_sketch, 'blk', scatter_dimension=1, tiled=True)  75 us
    another operation x13, other arithmetic, basis_from(): jax.scipy.linalg.solve_triangular(lower_factor, jnp.swapaxes(mixed_rows,...  67.2 us
    another operation x1, loops' own time, shards(): partial_sketch = lax.map(leaf_sketch, jnp.arange(local_rows))  19.8 us
    ppermute x4, waiting for transfers between devices, partner_2(): return lax.ppermute(block, axis, route)  19.7 us
  transfers between devices with their start and end apart: 10, of which 9 were waited for; matrix products, arithmetic and copies ran while one was open for 11% of the time, Pallas kernels for 0%

commit v1 on v0

--- a/solution.py
+++ b/solution.py
@@ -79,7 +79,8 @@
     gram_matrix = lax.psum(gram_part, "blk")
     basis_part = basis_from(gram_matrix, mixed_rows)
     proj_part = jnp.einsum("rbk,rbp->rkp", basis_part, sketch_rows, precision=highest)
-    leaf_proj = lax.psum(proj_part, "blk")
+    parts = lax.all_gather(proj_part, "blk", axis=0, tiled=False)
+    leaf_proj = parts.sum(axis=0)
     basis_low = lax.all_gather(basis_part.astype(jnp.bfloat16), "blk", axis=1, tiled=True)
     all_bases = lax.all_gather(basis_low, "leaf", axis=0, tiled=True)
     far_basis = all_bases[far_cols]

time: 681 us -> 752 us (1.10)
  waiting for transfers between devices: 388 us -> 451 us
  other arithmetic: 159 us -> 167 us
    psum x1 -> x0, waiting for transfers between devices: 93.2 us -> none  [shards(): leaf_proj = lax.psum(proj_part, 'blk')]
    all_gather x0 -> x1, waiting for transfers between devices: none -> 90.8 us  [shards(): parts = lax.all_gather(proj_part, 'blk', axis=0, tiled=False)]
    all_gather x1, waiting for transfers between devices: 0.01 us -> 71.2 us  [shards(): all_bases = lax.all_gather(basis_low, 'leaf', axis=0, tiled=True)]
    reduce_sum x0 -> x1, other arithmetic: none -> 7.93 us  [shards(): leaf_proj = parts.sum(axis=0)]
  transfers between devices with their start and end apart: 10 -> 10, of which waited for: 9 -> 10; matrix products, arithmetic and copies ran while one was open for 11% -> 2% of each run, Pallas kernels for 0% -> 0%
where the time goes in v1:
time: 752 us; the launch traced here: 750 us
  waiting for transfers between devices  451 us (60%)
  other arithmetic  167 us (22%)
  matrix products  33.8 us (4%)
  local copies, waits for them, and re-layouts  30.2 us (4%)
  loops' own time  24.6 us (3%)
  blocking collectives  18.4 us (2%)
  between operations  14.2 us (2%)
  starting transfers between devices  10.7 us (1%)
    psum x1, waiting for transfers between devices, shards(): gram_matrix = lax.psum(gram_part, 'blk')  109 us
    all_gather x1, waiting for transfers between devices, shards(): parts = lax.all_gather(proj_part, 'blk', axis=0, tiled=False)  90.8 us
    ppermute x1, waiting for transfers between devices, padded(): before = lax.ppermute(last, axis, up)  88.6 us
    another operation x19, other arithmetic, basis_from(): lower_factor = jnp.linalg.cholesky(gram_matrix)  79.7 us
    reduce_scatter x1, waiting for transfers between devices, shards(): lax.psum_scatter(partial_sketch, 'blk', scatter_dimension=1, tiled=True)  75 us
    all_gather x1, waiting for transfers between devices, shards(): all_bases = lax.all_gather(basis_low, 'leaf', axis=0, tiled=True)  71.2 us
    another operation x13, other arithmetic, basis_from(): jax.scipy.linalg.solve_triangular(lower_factor, jnp.swapaxes(mixed_rows,...  67.8 us
    another operation x1, loops' own time, shards(): partial_sketch = lax.map(leaf_sketch, jnp.arange(local_rows))  19.8 us
  transfers between devices with their start and end apart: 10, of which 10 were waited for; matrix products, arithmetic and copies ran while one was open for 2% of the time, Pallas kernels for 0%

profile of v1, /device:TPU:22, one launch (start us, length us, event | category | flops | bytes accessed | tf_op | source)
XLA Modules:
  0.0 750.5 jit_solution(17221751738433635304)
XLA Ops:
  7.2 3.2 collective-permute-start
  10.4 2.7 collective-permute-start.1
  13.1 88.6 %collective-permute-done = bf16[8,512,512]{2,1,0:T(8,128)(2,1)} collective-permute-done((bf16[8,512,512]{2,1,0:T(8,128)(2,1)}, bf16[8,512,512]{2,1,0:T(8,128)(2,1)}, u32[]{:S(2)}, u32[]{:S(2)}) %collective-permute-start) | collective-permute-done | bytes 4194336 | tf_op jit(solution)/shard_map/ppermute | solution.py:19
  101.7 2.9 collective-permute-done.1
  104.7 10.8 %pad_maximum_fusion = bf16[24,512,512]{2,1,0:T(8,128)(2,1)} fusion(bf16[8,512,512]{2,1,0:T(8,128)(2,1)} %collective-permute-done.1, bf16[8,512,512]{2,1,0:T(8,128)(2,1)} %param.17, bf16[8,512,512]{2,1,0:T(8,128)(2,1)} %collective-permute-done), kind=kLoop, calls=%fused_computation.9 | loop fusion | flops 12582912 | bytes 25165824 | tf_op jit(solution)/shard_map/concatenate | solution.py:21
  115.4 60.4 %while.10 = (s32[]{:T(128)}, f32[8,512,512]{2,1,0:T(8,128)}, s32[8]{0:T(128)S(1)}, s32[8]{0:T(128)S(1)}, s32[]{:T(128)}, /*index=5*/bf16[8,1,512,512]{3,2,1,0:T(...) while((s32[]{:T(128)}, f32[8,512,512]{2,1,0:T(8,128)}, ...), condition=%wide.region_3.4_spmd, body=%wide.region_0.3_spmd.sunk | while | flops 268435456 | bytes 4195627 | solution.py:75
  119.1 2.8 conditional.2
  120.3 1.6 convolution_bitcast_fusion
  121.9 1.1 constant_dynamic-update-slice_fusion.2
  126.7 2.8 conditional.2
  127.9 1.6 convolution_bitcast_fusion
  134.2 2.8 conditional.2
  135.4 1.6 convolution_bitcast_fusion
  137.0 1.1 constant_dynamic-update-slice_fusion.2
  141.7 2.8 conditional.2
  142.9 1.6 convolution_bitcast_fusion
  144.5 1.1 constant_dynamic-update-slice_fusion.2
  149.3 2.8 conditional.2
  150.4 1.6 convolution_bitcast_fusion
  152.1 1.1 constant_dynamic-update-slice_fusion.2
  156.8 2.8 conditional.2
  158.0 1.6 convolution_bitcast_fusion
  159.6 1.1 constant_dynamic-update-slice_fusion.2
  164.4 2.8 conditional.2
  165.6 1.6 convolution_bitcast_fusion
  167.2 1.1 constant_dynamic-update-slice_fusion.2
  171.9 2.8 conditional.2
  173.1 1.6 convolution_bitcast_fusion
  174.7 1.1 constant_dynamic-update-slice_fusion.2
  175.9 75.0 %reduce-scatter.2.cloned.1.call-done = f32[8,32,512]{2,1,0:T(8,128)} async-done(((f32[8,512,512]{2,1,0:T(8,128)}), f32[8,32,512]{2,1,0:T(8,128)}) %reduce-scatter.2.cloned.1.call-update) | async-done | bytes 524304 | tf_op jit(solution)/shard_map/reduce_scatter | solution.py:76
  250.8 1.6 fusion.20
  252.5 1.3 fusion.69
  253.9 108.8 %all-reduce.2.cloned.1.call-done = f32[8,64,64]{1,2,0:T(8,128)} async-done(((f32[8,64,64]{1,2,0:T(8,128)}), f32[8,64,64]{1,2,0:T(8,128)}) %all-reduce.2.cloned.1.call-update) | async-done | bytes 131088 | tf_op jit(solution)/shard_map/psum | solution.py:79
  362.7 1.1 copy.31
  364.8 46.9 %custom-call.17 = f32[8,64,64]{2,1,0:T(8,128)S(1)} custom-call(f32[8,64,64]{2,1,0:T(8,128)S(1)} %fusion.13), custom_call_target="Cholesky" | custom-call | tf_op jit(solution)/shard_map/jit(cholesky)/cholesky | solution.py:36
  411.9 39.3 %custom-call.18 = f32[8,1,64,64]{2,3,1,0:T(8,128)S(1)} custom-call(f32[8,1,64,64]{3,2,1,0:T(8,128)S(1)} %select_bitcast_fusion), custom_call_target="InvertDiagBlocksLowerTriangular" | custom-call | tf_op jit(solution)/shard_map/jit(_solve_triangular)/vmap()/triangular_solve | solution.py:37
  451.7 18.4 %all_gather.12 = bf16[8,512,64]{2,1,0:T(8,128)(2,1)S(1)} all-gather(bf16[8,32,64]{2,1,0:T(8,128)(2,1)S(1)} %convert_bitcast_fusion), channel_id=1, replica_groups=mesh['leaf'=16,'blk'=16] {'blk'}, dimensions={1}, use_global_device_ids=true | all-gather | bytes 557056 | tf_op jit(solution)/shard_map/all_gather | solution.py:84
  470.0 1.1 copy.33
  471.4 3.1 fusion.70
  474.6 71.2 %all-gather.4.cloned.1.call-done = bf16[128,512,64]{1,2,0:T(8,128)(2,1)} async-done(((bf16[8,512,64]{1,2,0:T(8,128)(2,1)}), bf16[128,512,64]{1,2,0:T(8,128)(2,1)}) %all-gather.4.cloned.1.call-update) | async-done | bytes 8388624 | tf_op jit(solution)/shard_map/all_gather | solution.py:85
  545.8 4.0 gather_fusion
  549.8 3.6 fusion.5
  553.3 90.8 %all-gather.6.cloned.1.call-done = f32[128,64,512]{2,1,0:T(8,128)} async-done(((f32[8,64,512]{2,1,0:T(8,128)}), f32[128,64,512]{2,1,0:T(8,128)}) %all-gather.6.cloned.1.call-update) | async-done | bytes 16777232 | tf_op jit(solution)/shard_map/all_gather | solution.py:82
  644.1 7.9 %reduce_sum.9 = f32[8,64,512]{2,1,0:T(8,128)S(1)} reduce(f32[16,8,64,512]{3,2,1,0:T(8,128)} %bitcast.137, f32[]{:T(128)} %constant.126.clone.1), dimensions={0}, to_apply=%region_8.9 | reduce | flops 3932160 | bytes 17825796 | tf_op jit(solution)/shard_map/reduce_sum | solution.py:83
  652.1 1.1 fusion.71
  653.6 5.8 cholesky.127
  660.8 5.5 custom-call.19
  666.3 1.1 fusion.43
  667.4 1.4 fusion.65
  668.8 1.2 collective-permute-start.2
  671.6 1.7 collective-permute-done.2
  674.0 5.8 cholesky.138
  681.1 4.9 custom-call.23
  687.6 5.0 collective-permute-done.3
  693.4 5.8 cholesky.149
  700.6 4.9 custom-call.24
  707.2 3.2 collective-permute-done.4
  711.1 5.8 cholesky.160
  718.2 4.9 custom-call.25
  723.7 1.5 collective-permute-start.5
  725.5 4.1 collective-permute-done.5
  730.2 5.8 cholesky.171
  737.4 4.9 custom-call.26
  742.9 1.1 convolution_multiply_fusion
  (107 shorter events, 33.1 us)
Async XLA Ops:
  7.2 243.7 %copy-start = (f32[512,64]{0,1:T(8,128)S(1)}, f32[512,64]{0,1:T(8,128)}, u32[]{:S(2)}) copy-start(f32[512,64]{0,1:T(8,128)} %param.18) | copy-start | bytes 393220
  7.2 243.7 %reduce-scatter.2.cloned.1.call-start = ((), (), s32[]{:S(2)}) async-start(), calls=%async_computation.1 | async-start | bytes 8912896 | tf_op jit(solution)/shard_map/reduce_scatter | solution.py:76
  7.2 94.5 %collective-permute-start = (bf16[8,512,512]{2,1,0:T(8,128)(2,1)}, bf16[8,512,512]{2,1,0:T(8,128)(2,1)}, u32[]{:S(2)}, u32[]{:S(2)}) collective-permute-start(bf16[8,512,512]{2,1,0:T(8,128)(2,1)} %param.17), channel_id=1, source_target_pairs={{0,16},{16,32},{32,48},{48,64},{64,80},{80,96},{96,112},{112,128},... | collective-permute-start | bytes 12582920 | tf_op jit(solution)/shard_map/ppermute | solution.py:19
  10.4 94.2 %collective-permute-start.1 = (bf16[8,512,512]{2,1,0:T(8,128)(2,1)}, bf16[8,512,512]{2,1,0:T(8,128)(2,1)}, u32[]{:S(2)}, u32[]{:S(2)}) collective-permute-start(bf16[8,512,512]{2,1,0:T(8,128)(2,1)} %param.17), channel_id=1, source_target_pairs={{16,0},{32,16},{48,32},{64,48},{80,64},{96,80},{112,96},{128,112},... | collective-permute-start | bytes 12582920 | tf_op jit(solution)/shard_map/ppermute | solution.py:20
  13.1 102.3 %copy-start.1 = (s32[8]{0:T(128)S(1)}, s32[8]{0:T(128)}, u32[]{:S(2)}) copy-start(s32[8]{0:T(128)} %param.16) | copy-start | bytes 100
  13.1 102.3 %copy-start.2 = (s32[8,1]{0,1:T(1,128)S(1)}, s32[8,1]{0,1:T(1,128)}, u32[]{:S(2)}) copy-start(s32[8,1]{0,1:T(1,128)} %param.15) | copy-start | bytes 100
  175.8 298.8 %copy-start.3 = (s32[8,1]{0,1:T(1,128)S(1)}, s32[8,1]{0,1:T(1,128)}, u32[]{:S(2)}) copy-start(s32[8,1]{0,1:T(1,128)} %param.20) | copy-start | bytes 100
  175.8 186.9 %all-reduce.2.cloned.1.call-start = ((), (), s32[]{:S(2)}) async-start(), calls=%async_computation.2 | async-start | bytes 524288 | tf_op jit(solution)/shard_map/psum | solution.py:79
  253.8 292.0 %all-gather.4.cloned.1.call-start = ((), (), s32[]{:S(2)}) async-start(), calls=%async_computation.3 | async-start | bytes 8912896 | tf_op jit(solution)/shard_map/all_gather | solution.py:85
  471.2 173.0 %all-gather.6.cloned.1.call-start = ((), (), s32[]{:S(2)}) async-start(), calls=%async_computation.4 | async-start | bytes 17825792 | tf_op jit(solution)/shard_map/all_gather | solution.py:82
  668.8 4.5 collective-permute-start.2
  686.6 6.1 collective-permute-start.3
  706.0 4.4 collective-permute-start.4
  723.7 5.9 collective-permute-start.5
Sparse Core Ops, SparseCore 0:
  175.9 74.8 reduce-scatter.1
  253.9 108.7 all-reduce.1
  471.3 74.4 all-gather.3
  547.5 96.6 all-gather.5
